TPU v7x, 32 devices: a whole 2x2x4 slice. The times are simulated.
32 devices in a mesh: fsdp: 8 (over y, x, core), ep: 4 (over z).
Axes of the slice: x: 2, y: 2, z: 4, core: 2. Of those that a mesh axis runs over, the one named last changes fastest.
Arguments:
- hidden: bfloat16 [2048, 8192], P('fsdp', 'ep'), may hold values from -6 to 6
- w_down: bfloat16 [6144, 2, 8192], P('fsdp', None, 'ep'), may hold values from -0.0625 to 0.0625
- route_ids: int32 [1024, 2], P('fsdp'), may hold values from 0 to 7, as said below
- probs: float32 [1024, 2], P('fsdp'), may hold values from 0.1 to 0.9
- grad_out: bfloat16 [1024, 6144], P('fsdp', 'ep'), may hold values from -6 to 6
Outputs:
- output: bfloat16 [1024, 6144], P('fsdp', 'ep')
- grad_hidden: bfloat16 [2048, 8192], P('fsdp', 'ep')
- grad_weight: bfloat16 [6144, 2, 8192], P('fsdp', None, 'ep')
- grad_probs: float32 [1024, 2], P('fsdp')
Inputs may be any that keep to these rules, and one draw needn't show every extreme that they name: `route_ids`: each token names 2 different experts. Within one panel's 128 tokens, experts 0 and 1 are each named by 1 to 128 tokens, and in some panel both are named by all 128 tokens.
All inputs are finite; a program needn't handle non-finite values.
Results may differ from a plain program's by a relative error of at most 0.012.
Values may be sent and summed in bfloat16 or wider, within the bound.
A program may use at most 384 MiB of HBM per device.

v0:
```python
import jax
import jax.numpy as jnp
from jax import lax
from jax.sharding import PartitionSpec as P

BLOCK = 128


def route_layout(route_part, prob_part, expert_count, block_rows, row_count):
    token_count = route_part.shape[0]
    experts = jnp.arange(expert_count, dtype=jnp.int32)
    hits = (route_part[:, :, None] == experts[None, None, :]).astype(jnp.int32)
    named = jnp.sum(hits, axis=1)
    counts = jnp.sum(named, axis=0)
    ranks = jnp.cumsum(named, axis=0) - named
    padded = (counts + block_rows - 1) // block_rows * block_rows
    offsets = jnp.cumsum(padded) - padded
    row_of = jnp.sum(hits * (offsets[None, None, :] + ranks[:, None, :]), axis=2)
    valid = jnp.sum(hits, axis=2)
    starts = jnp.arange(row_count // block_rows, dtype=jnp.int32) * block_rows
    inside = (starts[:, None] >= offsets[None, :]) & (starts[:, None] < (offsets + padded)[None, :])
    block_exp = jnp.sum(jnp.where(inside, experts[None, :] + 1, 0), axis=1) - 1
    target = jnp.where(valid > 0, row_of, row_count).reshape(-1)
    token_index = jnp.broadcast_to(
        jnp.arange(token_count, dtype=jnp.int32)[:, None], route_part.shape
    ).reshape(-1)
    row_tok = jnp.zeros((row_count,), jnp.int32).at[target].set(token_index, mode="drop")
    row_live = (
        jnp.zeros((row_count,), jnp.int32).at[target].set(jnp.ones_like(token_index), mode="drop")
    )
    row_prob = (
        jnp.zeros((row_count,), prob_part.dtype).at[target].set(prob_part.reshape(-1), mode="drop")
    )
    return (row_of, valid, block_exp, row_tok, row_live, row_prob)


def local(hidden, w_down, route_ids, probs, grad_out):
    row_count, unit_count = hidden.shape
    expert_count = w_down.shape[1]
    block_count = row_count // BLOCK
    row_of, valid, block_exp, row_tok, row_live, row_prob = route_layout(
        route_ids, probs, expert_count, BLOCK, row_count
    )
    safe_exp = jnp.maximum(block_exp, 0)
    prob_valid = probs * valid.astype(jnp.float32)
    full_grads = lax.all_gather(grad_out, "ep", axis=1, tiled=True)
    model_width = full_grads.shape[1]
    routed = jnp.where(row_live[:, None] > 0, full_grads[row_tok], jnp.zeros((), jnp.bfloat16))
    scaled = (row_prob[:, None] * routed.astype(jnp.float32)).astype(jnp.bfloat16)
    hid_blocks = hidden.reshape(block_count, BLOCK, unit_count)
    routed_blocks = routed.reshape(block_count, BLOCK, model_width)
    row_exp = jnp.repeat(block_exp, BLOCK)
    member = (row_exp[:, None] == jnp.arange(expert_count, dtype=jnp.int32)[None, :]).astype(
        jnp.bfloat16
    )
    masked_hid = hidden[:, None, :] * member[:, :, None]
    piece = lax.all_gather(w_down, "fsdp", axis=0, tiled=True)
    width = piece.shape[0]
    chosen = jnp.take(piece, safe_exp, axis=1)
    out_rows = jnp.einsum(
        "bri,dbi->brd", hid_blocks, chosen, preferred_element_type=jnp.float32
    ).reshape(row_count, width)
    back_total = jnp.einsum(
        "brd,dbi->bri", routed_blocks, chosen, preferred_element_type=jnp.float32
    )
    combined = jnp.sum(prob_valid[:, :, None] * out_rows[row_of], axis=1)
    out_total = combined
    out_total, back_total = (out_total, back_total)
    grad_weight = lax.psum_scatter(
        jnp.einsum("rd,rei->dei", scaled, masked_hid, preferred_element_type=jnp.float32).astype(
            jnp.bfloat16
        ),
        "fsdp",
        scatter_dimension=0,
        tiled=True,
    )
    output = lax.psum_scatter(out_total.astype(jnp.bfloat16), "ep", scatter_dimension=1, tiled=True)
    hidden_back = back_total.reshape(row_count, unit_count)
    grad_hidden = (row_prob[:, None] * hidden_back).astype(jnp.bfloat16)
    row_dot = jnp.sum(hidden.astype(jnp.float32) * hidden_back, axis=1)
    prob_terms = valid.astype(jnp.float32) * row_dot[row_of]
    grad_probs = lax.psum(prob_terms, "ep")
    return (output, grad_hidden, grad_weight, grad_probs)


def solution(mesh):
    placed = (
        P("fsdp", "ep"),
        P("fsdp", None, "ep"),
        P("fsdp", None),
        P("fsdp", None),
        P("fsdp", "ep"),
    )
    return jax.shard_map(
        local,
        mesh=mesh,
        in_specs=placed,
        out_specs=(P("fsdp", "ep"), P("fsdp", "ep"), P("fsdp", None, "ep"), P("fsdp", None)),
        check_vma=False,
    )
```

profile of v0, /device:TPU:4, one launch (start us, length us, event | category | flops | bytes accessed | tf_op | source)
XLA Modules:
  0.0 634.3 jit_solution(14992355778642910269)
XLA Ops:
  7.9 8.4 %copy.21 = bf16[768,2,2048]{2,0,1:T(8,128)(2,1)} copy(bf16[768,2,2048]{2,1,0:T(2,128)(2,1)} %param.6) | data formatting | bytes 12582912 | tf_op args[1]
  23.2 24.7 %all-gather.5.cloned.1.call-done = bf16[128,6144]{1,0:T(8,128)(2,1)} async-done(((bf16[128,1536]{1,0:T(8,128)(2,1)}), bf16[128,6144]{1,0:T(8,128)(2,1)}) %all-gather.5.cloned.1.call-update) | async-done | bytes 1572880 | tf_op jit(solution)/shard_map/all_gather | solution.py:46
  47.9 7.1 %gather_fusion.1 = bf16[256,6144]{1,0:T(8,128)(2,1)S(1)} fusion(bf16[128,6144]{1,0:T(8,128)(2,1)} %all-gather.5.cloned.1.call-done, s32[1024]{0:T(1024)S(1)} %pad_clamp_fusion), kind=kCustom, calls=%fused_computation.1 | custom fusion | bytes 6292480 | tf_op jit(solution)/shard_map/gather | solution.py:48
  55.0 25.2 %convolution_convert_fusion = bf16[6144,2,2048]{2,0,1:T(8,128)(2,1)} fusion(bf16[256,6144]{1,0:T(8,128)(2,1)S(1)} %gather_fusion.1, f32[256]{0:T(256)S(1)} %scatter_custom_fusion, pred[256]{0:T(512)(128)(4,1)S(1)} %broadcast_compare_fusion, bf16[256,2]{0,1:T(2,128)(2,1)S(1)} %compare_convert_fusion, bf16[256,2048]{1,0:T(8,128)(2,1)} %param.5), kind=kOutput, calls=%fused_computation.31 | convolution fusion | flops 12920553472 | bytes 54528256 | tf_op jit(solution)/shard_map/rd,rei->dei/dot_general | solution.py:70
  81.9 198.1 %all-gather.3.cloned.1.call-done = bf16[6144,2,2048]{2,0,1:T(8,128)(2,1)} async-done(((bf16[768,2,2048]{2,0,1:T(8,128)(2,1)}), bf16[6144,2,2048]{2,0,1:T(8,128)(2,1)}) %all-gather.3.cloned.1.call-update) | async-done | bytes 50331664 | tf_op jit(solution)/shard_map/all_gather | solution.py:57
  280.0 40.8 %fusion.28 = (bf16[512,2,2048]{2,0,1:T(8,128)(2,1)}, bf16[512,2,2048]{2,0,1:T(8,128)(2,1)}, bf16[512,2,2048]{2,0,1:T(8,128)(2,1)}, bf16[512,2,2048]{2,0,1:T(8,12...) fusion(bf16[6144,2,2048]{2,0,1:T(8,128)(2,1)} %all-gather.3.clo, ...), kind=kLoop, calls=%fused_computation.108 | loop fusion | bytes 100663296 | tf_op jit(solution)/shard_map/jit(_take)/gather | solution.py:59
  323.9 9.5 %while.12 = (s32[]{:T(128)}, bf16[512,2,2048]{2,0,1:T(8,128)(2,1)}, s32[2,1]{0,1:T(1,128)S(1)}, bf16[2,512,2048]{2,1,0:T(8,128)(2,1)}, s32[]{:T(128)}) while((s32[]{:T(128)}, bf16[512,2,2048]{2,0,1:T(8,128)(2,1)}, s32[2,1]{0,1:T(1,128)S(1)}, bf16[2,512,2048]{2,1,0:T(8,128)(2,1)}, s32[]{:T(128)}) %tuple.161), condition=%wide.while_cond, body=%wide.while_body.sunk | while | flops 2 | bytes 4195401 | solution.py:59
  324.5 4.2 bitcast_dynamic-update-slice_fusion.36
  329.2 4.2 bitcast_dynamic-update-slice_fusion.36
  336.4 9.7 %while.13 = (s32[]{:T(128)}, bf16[512,2,2048]{2,0,1:T(8,128)(2,1)}, s32[2,1]{0,1:T(1,128)S(1)}, bf16[2,512,2048]{2,1,0:T(8,128)(2,1)}, s32[]{:T(128)}) while((s32[]{:T(128)}, bf16[512,2,2048]{2,0,1:T(8,128)(2,1)}, s32[2,1]{0,1:T(1,128)S(1)}, bf16[2,512,2048]{2,1,0:T(8,128)(2,1)}, s32[]{:T(128)}) %tuple.205), condition=%wide.while_cond.1, body=%wide.while_body.1.sunk | while | flops 2 | bytes 4195401 | solution.py:59
  337.0 4.3 bitcast_dynamic-update-slice_fusion.37
  341.8 4.3 bitcast_dynamic-update-slice_fusion.37
  348.7 8.9 %while.14 = (s32[]{:T(128)}, bf16[512,2,2048]{2,0,1:T(8,128)(2,1)}, s32[2,1]{0,1:T(1,128)S(1)}, bf16[2,512,2048]{2,1,0:T(8,128)(2,1)}, s32[]{:T(128)}) while((s32[]{:T(128)}, bf16[512,2,2048]{2,0,1:T(8,128)(2,1)}, s32[2,1]{0,1:T(1,128)S(1)}, bf16[2,512,2048]{2,1,0:T(8,128)(2,1)}, s32[]{:T(128)}) %tuple.206), condition=%wide.while_cond.2, body=%wide.while_body.2.sunk | while | flops 2 | bytes 4195401 | solution.py:59
  353.6 3.9 bitcast_dynamic-update-slice_fusion.38
  360.1 8.8 %while.15 = (s32[]{:T(128)}, bf16[512,2,2048]{2,0,1:T(8,128)(2,1)}, s32[2,1]{0,1:T(1,128)S(1)}, bf16[2,512,2048]{2,1,0:T(8,128)(2,1)}, s32[]{:T(128)}) while((s32[]{:T(128)}, bf16[512,2,2048]{2,0,1:T(8,128)(2,1)}, s32[2,1]{0,1:T(1,128)S(1)}, bf16[2,512,2048]{2,1,0:T(8,128)(2,1)}, s32[]{:T(128)}) %tuple.207), condition=%wide.while_cond.3, body=%wide.while_body.3.sunk | while | flops 2 | bytes 4195401 | solution.py:59
  360.7 3.8 bitcast_dynamic-update-slice_fusion.39
  365.1 3.9 bitcast_dynamic-update-slice_fusion.39
  371.5 8.8 %while.16 = (s32[]{:T(128)}, bf16[512,2,2048]{2,0,1:T(8,128)(2,1)}, s32[2,1]{0,1:T(1,128)S(1)}, bf16[2,512,2048]{2,1,0:T(8,128)(2,1)}, s32[]{:T(128)}) while((s32[]{:T(128)}, bf16[512,2,2048]{2,0,1:T(8,128)(2,1)}, s32[2,1]{0,1:T(1,128)S(1)}, bf16[2,512,2048]{2,1,0:T(8,128)(2,1)}, s32[]{:T(128)}) %tuple.208), condition=%wide.while_cond.4, body=%wide.while_body.4.sunk | while | flops 2 | bytes 4195401 | solution.py:59
  372.1 3.8 bitcast_dynamic-update-slice_fusion.40
  382.8 9.1 %while.17 = (s32[]{:T(128)}, bf16[512,2,2048]{2,0,1:T(8,128)(2,1)}, s32[2,1]{0,1:T(1,128)S(1)}, bf16[2,512,2048]{2,1,0:T(8,128)(2,1)}, s32[]{:T(128)}) while((s32[]{:T(128)}, bf16[512,2,2048]{2,0,1:T(8,128)(2,1)}, s32[2,1]{0,1:T(1,128)S(1)}, bf16[2,512,2048]{2,1,0:T(8,128)(2,1)}, s32[]{:T(128)}) %tuple.209), condition=%wide.while_cond.5, body=%wide.while_body.5.sunk | while | flops 2 | bytes 4195401 | solution.py:59
  383.4 4.0 bitcast_dynamic-update-slice_fusion.41
  388.0 3.9 bitcast_dynamic-update-slice_fusion.41
  394.5 9.2 %while.18 = (s32[]{:T(128)}, bf16[512,2,2048]{2,0,1:T(8,128)(2,1)}, s32[2,1]{0,1:T(1,128)S(1)}, bf16[2,512,2048]{2,1,0:T(8,128)(2,1)}, s32[]{:T(128)}) while((s32[]{:T(128)}, bf16[512,2,2048]{2,0,1:T(8,128)(2,1)}, s32[2,1]{0,1:T(1,128)S(1)}, bf16[2,512,2048]{2,1,0:T(8,128)(2,1)}, s32[]{:T(128)}) %tuple.210), condition=%wide.while_cond.6, body=%wide.while_body.6.sunk | while | flops 2 | bytes 4195401 | solution.py:59
  395.1 3.9 bitcast_dynamic-update-slice_fusion.42
  399.6 4.1 bitcast_dynamic-update-slice_fusion.42
  406.2 8.9 %while.19 = (s32[]{:T(128)}, bf16[512,2,2048]{2,0,1:T(8,128)(2,1)}, s32[2,1]{0,1:T(1,128)S(1)}, bf16[2,512,2048]{2,1,0:T(8,128)(2,1)}, s32[]{:T(128)}) while((s32[]{:T(128)}, bf16[512,2,2048]{2,0,1:T(8,128)(2,1)}, s32[2,1]{0,1:T(1,128)S(1)}, bf16[2,512,2048]{2,1,0:T(8,128)(2,1)}, s32[]{:T(128)}) %tuple.211), condition=%wide.while_cond.7, body=%wide.while_body.7.sunk | while | flops 2 | bytes 4195401 | solution.py:59
  406.8 3.9 bitcast_dynamic-update-slice_fusion.43
  411.2 3.8 bitcast_dynamic-update-slice_fusion.43
  417.5 8.8 %while.20 = (s32[]{:T(128)}, bf16[512,2,2048]{2,0,1:T(8,128)(2,1)}, s32[2,1]{0,1:T(1,128)S(1)}, bf16[2,512,2048]{2,1,0:T(8,128)(2,1)}, s32[]{:T(128)}) while((s32[]{:T(128)}, bf16[512,2,2048]{2,0,1:T(8,128)(2,1)}, s32[2,1]{0,1:T(1,128)S(1)}, bf16[2,512,2048]{2,1,0:T(8,128)(2,1)}, s32[]{:T(128)}) %tuple.212), condition=%wide.while_cond.8, body=%wide.while_body.8.sunk | while | flops 2 | bytes 4195401 | solution.py:59
  422.5 3.8 bitcast_dynamic-update-slice_fusion.44
  428.8 9.3 %while.21 = (s32[]{:T(128)}, bf16[512,2,2048]{2,0,1:T(8,128)(2,1)}, s32[2,1]{0,1:T(1,128)S(1)}, bf16[2,512,2048]{2,1,0:T(8,128)(2,1)}, s32[]{:T(128)}) while((s32[]{:T(128)}, bf16[512,2,2048]{2,0,1:T(8,128)(2,1)}, s32[2,1]{0,1:T(1,128)S(1)}, bf16[2,512,2048]{2,1,0:T(8,128)(2,1)}, s32[]{:T(128)}) %tuple.213), condition=%wide.while_cond.9, body=%wide.while_body.9.sunk | while | flops 2 | bytes 4195401 | solution.py:59
  429.4 4.1 bitcast_dynamic-update-slice_fusion.45
  434.1 4.0 bitcast_dynamic-update-slice_fusion.45
  440.7 8.9 %while.22 = (s32[]{:T(128)}, bf16[512,2,2048]{2,0,1:T(8,128)(2,1)}, s32[2,1]{0,1:T(1,128)S(1)}, bf16[2,512,2048]{2,1,0:T(8,128)(2,1)}, s32[]{:T(128)}) while((s32[]{:T(128)}, bf16[512,2,2048]{2,0,1:T(8,128)(2,1)}, s32[2,1]{0,1:T(1,128)S(1)}, bf16[2,512,2048]{2,1,0:T(8,128)(2,1)}, s32[]{:T(128)}) %tuple.214), condition=%wide.while_cond.10, body=%wide.while_body.10.sunk | while | flops 2 | bytes 4195401 | solution.py:59
  441.2 3.8 bitcast_dynamic-update-slice_fusion.46
  445.6 3.9 bitcast_dynamic-update-slice_fusion.46
  452.1 8.9 %while.23 = (s32[]{:T(128)}, bf16[512,2,2048]{2,0,1:T(8,128)(2,1)}, s32[2,1]{0,1:T(1,128)S(1)}, bf16[2,512,2048]{2,1,0:T(8,128)(2,1)}, s32[]{:T(128)}) while((s32[]{:T(128)}, bf16[512,2,2048]{2,0,1:T(8,128)(2,1)}, s32[2,1]{0,1:T(1,128)S(1)}, bf16[2,512,2048]{2,1,0:T(8,128)(2,1)}, s32[]{:T(128)}) %tuple.215), condition=%wide.while_cond.11, body=%wide.while_body.11.sunk | while | flops 2 | bytes 4195401 | solution.py:59
  452.7 3.9 bitcast_dynamic-update-slice_fusion.47
  457.1 3.8 bitcast_dynamic-update-slice_fusion.47
  460.9 4.9 bitcast_dynamic-update-slice_fusion.23
  506.1 25.7 %fusion.1 = f32[2,6144,128]{1,2,0:T(8,128)} fusion(bf16[2,128,2048]{2,1,0:T(8,128)(2,1)S(1)} %bitcast.149, bf16[6144,2,2048]{2,0,1:T(8,128)(2,1)} %bitcast_dynamic-update-slice_fusion.12, pred[2]{0:T(512)(128)(4,1)S(1)} %maximum_compare_fusion), kind=kOutput, calls=%fused_computation.33 | convolution fusion | flops 6467616768 | bytes 57671680 | tf_op jit(solution)/shard_map/bri,dbi->brd/dot_general | solution.py:60
  531.8 10.9 %gather_fusion = f32[256,6144]{1,0:T(8,128)} fusion(f32[256,6144]{1,0:T(8,128)} %bitcast.147, s32[1024]{0:T(1024)S(1)} %copy-done.14), kind=kCustom, calls=%fused_computation | custom fusion | bytes 12583936 | tf_op jit(solution)/shard_map/gather | solution.py:66
  542.8 8.6 %reshape.505 = f32[128,2,6144]{2,1,0:T(2,128)} reshape(f32[256,6144]{1,0:T(8,128)} %gather_fusion) | data formatting | bytes 12582912 | tf_op jit(solution)/shard_map/gather | solution.py:66
  551.4 20.4 %fusion = f32[2,128,2048]{2,1,0:T(8,128)} fusion(bf16[6144,2,2048]{2,0,1:T(8,128)(2,1)} %bitcast_dynamic-update-slice_fusion.12, pred[2]{0:T(512)(128)(4,1)S(1)} %maximum_compare_fusion, bf16[2,128,6144]{2,1,0:T(8,128)(2,1)S(1)} %bitcast.148, pred[2,128]{1,0:T(4,128)(4,1)S(1)} %copy-done.22), kind=kOutput, calls=%fused_computation.32 | convolution fusion | flops 6469189632 | bytes 55574784 | tf_op jit(solution)/shard_map/brd,dbi->bri/dot_general | solution.py:63
  577.5 11.9 %multiply_reduce_fusion = bf16[128,6144]{1,0:T(8,128)(2,1)} fusion(f32[128,2,6144]{2,1,0:T(2,128)} %reshape.505, f32[128,2]{1,0:T(8,128)S(1)} %copy.20), kind=kLoop, calls=%fused_computation.35 | loop fusion | flops 2359296 | bytes 7865344 | tf_op jit(solution)/shard_map/reduce_sum | solution.py:66
  589.4 12.6 %copy.30 = bf16[768,2,2048]{2,1,0:T(2,128)(2,1)} copy(bf16[768,2,2048]{2,0,1:T(8,128)(2,1)} %reduce-scatter.5.cloned.1.call-done) | data formatting | bytes 12582912
  602.0 14.4 %psum.7 = f32[128,2]{0,1:T(2,128)} all-reduce(f32[128,2]{0,1:T(2,128)S(1)} %get-tuple-element.225), channel_id=1, replica_groups=mesh['fsdp'=8,'ep'=4] {'ep'}, use_global_device_ids=true, to_apply=%region_14.15 | all-reduce | flops 256 | bytes 2048 | tf_op jit(solution)/shard_map/psum | solution.py:82
  616.5 10.8 %reduce-scatter.3.cloned.1.call-done = bf16[128,1536]{1,0:T(8,128)(2,1)} async-done(((bf16[128,6144]{1,0:T(8,128)(2,1)}), bf16[128,1536]{1,0:T(8,128)(2,1)}) %reduce-scatter.3.cloned.1.call-update) | async-done | bytes 393232 | tf_op jit(solution)/shard_map/reduce_scatter | solution.py:77
  (146 shorter events, 112.0 us)
Async XLA Ops:
  7.2 40.7 %all-gather.5.cloned.1.call-start = ((), (), s32[]{:S(2)}) async-start(), calls=%async_computation.4 | async-start | bytes 1966080 | tf_op jit(solution)/shard_map/all_gather | solution.py:46
  7.9 272.1 %all-gather.3.cloned.1.call-start = ((), (), s32[]{:S(2)}) async-start(), calls=%async_computation.2 | async-start | bytes 56623104 | tf_op jit(solution)/shard_map/all_gather | solution.py:57
  16.3 0.7 copy-start.21
  16.3 4.7 copy-start.19
  16.4 573.0 %reduce-scatter.5.cloned.1.call-start = ((), (), s32[]{:S(2)}) async-start(), calls=%async_computation.5 | async-start | bytes 56623104 | tf_op jit(solution)/shard_map/reduce_scatter | solution.py:69
  17.1 6.0 copy-start.17
  22.8 32.2 %copy-start.15 = (f32[256]{0:T(256)}, f32[256]{0:T(256)S(1)}, u32[]{:S(2)}) copy-start(f32[256]{0:T(256)S(1)} %scatter_custom_fusion) | copy-start | bytes 3076
  55.0 25.2 %copy-start.11 = (bf16[256,6144]{1,0:T(8,128)(2,1)}, bf16[256,6144]{1,0:T(8,128)(2,1)S(1)}, u32[]{:S(2)}) copy-start(bf16[256,6144]{1,0:T(8,128)(2,1)S(1)} %gather_fusion.1) | copy-start | bytes 9437188
  80.2 547.1 %reduce-scatter.3.cloned.1.call-start = ((), (), s32[]{:S(2)}) async-start(), calls=%async_computation.3 | async-start | bytes 1966080 | tf_op jit(solution)/shard_map/reduce_scatter | solution.py:77
  460.9 4.9 copy-start.1
  465.8 3.9 copy-start.2
  469.8 3.9 copy-start.3
  473.7 3.8 copy-start.4
  477.5 3.7 copy-start.5
  481.3 3.7 copy-start.6
  485.0 3.8 copy-start.7
  488.7 3.7 copy-start.8
  492.5 3.7 copy-start.9
  496.2 3.8 copy-start.10
  500.0 3.8 copy-start
  503.8 2.2 copy-start.13
  506.1 25.7 %copy-start.14 = (s32[1024]{0:T(1024)S(1)}, s32[1024]{0:T(1024)}, u32[]{:S(2)}) copy-start(s32[1024]{0:T(1024)} %pad_clamp_fusion.1) | copy-start | bytes 12292
  542.7 8.6 %copy-start.12 = (bf16[256,6144]{1,0:T(8,128)(2,1)S(1)}, bf16[256,6144]{1,0:T(8,128)(2,1)}, u32[]{:S(2)}) copy-start(bf16[256,6144]{1,0:T(8,128)(2,1)} %copy-done.11) | copy-start | bytes 9437188
  542.8 8.6 %copy-start.22 = (pred[2,128]{1,0:T(4,128)(4,1)S(1)}, pred[2,128]{1,0:T(4,128)(4,1)}, u32[]{:S(2)}) copy-start(pred[2,128]{1,0:T(4,128)(4,1)} %fusion.30) | copy-start | bytes 772
  551.3 20.4 %copy-start.16 = (f32[256]{0:T(256)S(1)}, f32[256]{0:T(256)}, u32[]{:S(2)}) copy-start(f32[256]{0:T(256)} %copy-done.15) | copy-start | bytes 3076
  574.9 2.4 copy-start.18
  574.9 2.5 copy-start.20
Sparse Core Ops, SparseCore 0:
  9.6 38.2 all-gather.4
  50.4 229.6 all-gather.2
  283.7 286.9 reduce-scatter.4
  589.5 37.7 reduce-scatter.2
where the time goes:
time: 643 us; the launch traced here: 634 us
  local copies, waits for them, and re-layouts  282 us (44%)
  waiting for transfers between devices  234 us (36%)
  matrix products  71.3 us (11%)
  other arithmetic  17 us (3%)
  between operations  14.5 us (2%)
  blocking collectives  14.4 us (2%)
    all_gather x1, waiting for transfers between devices, local(): piece = lax.all_gather(w_down, 'fsdp', axis=0, tiled=True)  198 us
    gather x48, local copies, waits for them, and re-layouts  109 us
    unnamed x73, local copies, waits for them, and re-layouts  98.4 us
    gather x1, local copies, waits for them, and re-layouts, local(): chosen = jnp.take(piece, safe_exp, axis=1)  40.8 us
    dot_general x1, matrix products, local(): jnp.einsum('bri,dbi->brd', hid_blocks, chosen, preferred_element_type=jnp...  25.7 us
    dot_general x1, matrix products, local(): jnp.einsum('rd,rei->dei', scaled, masked_hid, preferred_element_type=jnp....  25.2 us
    all_gather x1, waiting for transfers between devices, local(): full_grads = lax.all_gather(grad_out, 'ep', axis=1, tiled=True)  24.7 us
    dot_general x1, matrix products, local(): jnp.einsum('brd,dbi->bri', routed_blocks, chosen, preferred_element_type=...  20.4 us
  transfers between devices with their start and end apart: 4, of which 3 were waited for; matrix products, arithmetic and copies ran while one was open for 56% of the time, Pallas kernels for 0%

commit v1 on v0

v1 whole, which is shorter than its diff:
```python
import jax
import jax.numpy as jnp
from jax import lax
from jax.sharding import PartitionSpec as P

F32 = jnp.float32
BF16 = jnp.bfloat16


def route_maps(route_ids, probs, experts):
    tokens = route_ids.shape[0]
    names = jnp.arange(experts, dtype=jnp.int32)
    hits = (route_ids[:, :, None] == names[None, None, :]).astype(F32)
    named = jnp.sum(hits, axis=1)
    place = jnp.arange(tokens, dtype=jnp.int32)
    earlier = (place[None, :] < place[:, None]).astype(F32)
    rank = jnp.sum(earlier[:, :, None] * named[None, :, :], axis=1).astype(jnp.int32)
    token_prob = jnp.sum(hits * probs[:, :, None], axis=1)
    owns = (rank.T[:, :, None] == place[None, None, :]) & (named.T[:, :, None] > 0)
    return hits, token_prob, owns.astype(BF16)


def local(hidden, w_down, route_ids, probs, grad_out):
    rows, units = hidden.shape
    experts = w_down.shape[1]
    tokens = route_ids.shape[0]
    hits, token_prob, owns = route_maps(route_ids, probs, experts)
    hid_tok = jnp.einsum(
        "etr,erf->tef", owns, hidden.reshape(experts, tokens, units), preferred_element_type=F32
    )
    scaled = (token_prob[:, :, None] * hid_tok).astype(BF16)
    hid_all = lax.all_gather(scaled, "fsdp", axis=0, tiled=True)
    grads = lax.all_gather(grad_out, "ep", axis=1, tiled=True)
    grads = lax.all_to_all(grads, "fsdp", split_axis=1, concat_axis=0, tiled=True)
    back_part = jnp.einsum("td,def->tef", grads, w_down, preferred_element_type=F32).astype(BF16)
    back = lax.psum_scatter(back_part, "fsdp", scatter_dimension=0, tiled=True)
    part = jnp.einsum("tef,def->td", hid_all, w_down, preferred_element_type=F32).astype(BF16)
    part = lax.all_to_all(part, "fsdp", split_axis=0, concat_axis=1, tiled=True)
    output = lax.psum_scatter(part, "ep", scatter_dimension=1, tiled=True)
    grad_weight = jnp.einsum("td,tef->def", grads, hid_all, preferred_element_type=F32).astype(BF16)
    back = back.astype(F32)
    grad_tok = (token_prob[:, :, None] * back).astype(BF16)
    grad_hidden = jnp.einsum("etr,tef->erf", owns, grad_tok, preferred_element_type=F32)
    grad_hidden = grad_hidden.astype(BF16).reshape(rows, units)
    dots = jnp.sum(hid_tok * back, axis=2)
    grad_probs = lax.psum(jnp.sum(hits * dots[:, None, :], axis=2), "ep")
    return (output, grad_hidden, grad_weight, grad_probs)


def solution(mesh):
    placed = (
        P("fsdp", "ep"),
        P("fsdp", None, "ep"),
        P("fsdp", None),
        P("fsdp", None),
        P("fsdp", "ep"),
    )
    return jax.shard_map(
        local,
        mesh=mesh,
        in_specs=placed,
        out_specs=(P("fsdp", "ep"), P("fsdp", "ep"), P("fsdp", None, "ep"), P("fsdp", None)),
        check_vma=False,
    )
```

time: 643 us -> 298 us (0.46)
  local copies, waits for them, and re-layouts: 282 us -> 21.1 us
  waiting for transfers between devices: 234 us -> 163 us
  blocking collectives: 14.4 us -> 59.2 us
  matrix products: 71.3 us -> 35.8 us
  other arithmetic: 17 us -> 1.31 us
    gather x55 -> x0, local copies, waits for them, and re-layouts: 178 us -> none
    all_gather x2, waiting for transfers between devices: 223 us -> 94.2 us  [the longest x1 54.2 us: local(): hid_all = lax.all_gather(scaled, 'fsdp', axis=0, tiled=True)]
    unnamed x73 -> x13, local copies, waits for them, and re-layouts: 98.4 us -> 18.1 us
    reduce_scatter x2, waiting for transfers between devices: 10.8 us -> 68.5 us  [the longest x1 68.5 us: local(): back = lax.psum_scatter(back_part, 'fsdp', scatter_dimension=0, tiled=True)]
    all_to_all x0 -> x2, blocking collectives: none -> 46.6 us  [the longest x1 23.7 us: local(): lax.all_to_all(grads, 'fsdp', split_axis=1, concat_axis=0, tiled=True)]
    dot_general x3 -> x5, matrix products: 71.3 us -> 35.8 us  [the longest x1 12 us: local(): jnp.einsum('tef,def->td', hid_all, w_down, preferred_element_type=F32)]
    reduce_sum x5 -> x3, other arithmetic: 15.4 us -> 0.14 us  [the longest x1 0.1 us: route_maps(): jnp.sum(earlier[:, :, None] * named[None, :, :], axis=1).astype(jnp.int32)]
  transfers between devices with their start and end apart: 4 -> 4, of which waited for: 3 -> 3; matrix products, arithmetic and copies ran while one was open for 56% -> 10% of each run, Pallas kernels for 0% -> 0%
where the time goes in v1:
time: 298 us; the launch traced here: 295 us
  waiting for transfers between devices  163 us (55%)
  blocking collectives  59.2 us (20%)
  matrix products  35.8 us (12%)
  local copies, waits for them, and re-layouts  21.1 us (7%)
  between operations  13.8 us (5%)
    reduce_scatter x1, waiting for transfers between devices, local(): back = lax.psum_scatter(back_part, 'fsdp', scatter_dimension=0, tiled=True)  68.5 us
    all_gather x1, waiting for transfers between devices, local(): hid_all = lax.all_gather(scaled, 'fsdp', axis=0, tiled=True)  54.2 us
    all_gather x1, waiting for transfers between devices, local(): grads = lax.all_gather(grad_out, 'ep', axis=1, tiled=True)  40 us
    all_to_all x1, blocking collectives, local(): lax.all_to_all(grads, 'fsdp', split_axis=1, concat_axis=0, tiled=True)  23.7 us
    all_to_all x1, blocking collectives, local(): part = lax.all_to_all(part, 'fsdp', split_axis=0, concat_axis=1, tiled=True)  23 us
    unnamed x13, local copies, waits for them, and re-layouts  18.1 us
    psum x1, blocking collectives, local(): grad_probs = lax.psum(jnp.sum(hits * dots[:, None, :], axis=2), 'ep')  12.5 us
    dot_general x1, matrix products, local(): jnp.einsum('tef,def->td', hid_all, w_down, preferred_element_type=F32)  12 us
  transfers between devices with their start and end apart: 4, of which 3 were waited for; matrix products, arithmetic and copies ran while one was open for 10% of the time, Pallas kernels for 0%

profile of v1, /device:TPU:4, one launch (start us, length us, event | category | flops | bytes accessed | tf_op | source)
XLA Modules:
  0.0 294.8 jit_solution(3061528877056668230)
XLA Ops:
  7.2 0.0 copy-start
  7.2 0.0 all-gather.5.cloned.1.call-start
  7.2 0.7 all-gather.5.cloned.1.call-update
  7.9 0.0 reduce-scatter.5.cloned.1.call-start
  8.0 40.0 %all-gather.5.cloned.1.call-done = bf16[128,6144]{1,0:T(8,128)(2,1)} async-done(((bf16[128,1536]{1,0:T(8,128)(2,1)}), bf16[128,6144]{1,0:T(8,128)(2,1)}) %all-gather.5.cloned.1.call-update) | async-done | bytes 1572880 | tf_op jit(solution)/shard_map/all_gather | solution.py:33
  47.9 0.0 copy-start.5
  47.9 1.7 copy.50
  49.6 23.7 %all_to_all.38 = bf16[128,8,768]{2,0,1:T(8,128)(2,1)S(1)} all-to-all(bf16[128,8,768]{2,0,1:T(8,128)(2,1)S(1)} %bitcast.32), channel_id=1, replica_groups=mesh['fsdp'=8,'ep'=4] {'fsdp'}, dimensions={1} | all-to-all | bytes 3145728 | tf_op jit(solution)/shard_map/all_to_all | solution.py:34
  73.2 0.0 copy-start.2
  73.2 1.1 copy-done.2
  74.4 0.0 copy-done.5
  74.4 9.2 %fusion.4 = bf16[1024,2,2048]{2,0,1:T(8,128)(2,1)} fusion(bf16[1024,768,1]{1,0,2:T(8,128)(2,1)S(1)} %bitcast.34, bf16[768,2,2048]{2,1,0:T(2,128)(2,1)S(1)} %copy-done.5), kind=kOutput, calls=%fused_computation.5 | convolution fusion | flops 6446645248 | bytes 16252928 | tf_op jit(solution)/shard_map/td,def->tef/dot_general | solution.py:35
  83.6 0.0 copy-start.3
  83.6 0.0 reduce-scatter.5.cloned.1.call-update
  83.6 0.0 copy-start.4
  83.6 0.0 all-gather.3.cloned.1.call-start
  83.6 0.6 copy-done.3
  84.3 0.1 multiply_reduce_fusion
  84.4 68.5 %reduce-scatter.5.cloned.1.call-done = bf16[128,2,2048]{2,0,1:T(8,128)(2,1)} async-done(((bf16[1024,2,2048]{2,0,1:T(8,128)(2,1)}), bf16[128,2,2048]{2,0,1:T(8,128)(2,1)}) %reduce-scatter.5.cloned.1.call-update) | async-done | bytes 1048592 | tf_op jit(solution)/shard_map/reduce_scatter | solution.py:36
  152.9 0.0 copy-done
  152.9 1.8 fusion.8
  154.7 0.0 copy-done.4
  154.7 1.1 multiply_convert_fusion
  155.8 0.0 all-gather.3.cloned.1.call-update
  155.9 0.0 reduce-scatter.3.cloned.1.call-start
  155.9 54.2 %all-gather.3.cloned.1.call-done = bf16[1024,2,2048]{2,0,1:T(8,128)(2,1)} async-done(((bf16[128,2,2048]{2,0,1:T(8,128)(2,1)}), bf16[1024,2,2048]{2,0,1:T(8,128)(2,1)}) %all-gather.3.cloned.1.call-update) | async-done | bytes 8388624 | tf_op jit(solution)/shard_map/all_gather | solution.py:32
  210.1 12.0 %bitcast_convert_fusion = bf16[1024,768]{1,0:T(8,128)(2,1)S(1)} fusion(bf16[1024,2,2048]{2,0,1:T(8,128)(2,1)} %all-gather.3.cloned.1.call-done, bf16[768,2,2048]{2,1,0:T(2,128)(2,1)} %param.6), kind=kOutput, calls=%fused_computation.6 | convolution fusion | flops 6443237376 | bytes 16252928 | tf_op jit(solution)/shard_map/tef,def->td/dot_general | solution.py:37
  222.1 23.0 %all_to_all.39 = bf16[8,128,768]{2,1,0:T(8,128)(2,1)S(1)} all-to-all(bf16[8,128,768]{2,1,0:T(8,128)(2,1)S(1)} %bitcast.37), channel_id=1, replica_groups=mesh['fsdp'=8,'ep'=4] {'fsdp'}, dimensions={0} | all-to-all | bytes 3145728 | tf_op jit(solution)/shard_map/all_to_all | solution.py:38
  245.1 0.0 copy-start.1
  245.1 1.3 copy.40
  246.4 0.0 reduce-scatter.3.cloned.1.call-update
  246.4 12.5 %psum.7 = f32[128,2]{0,1:T(2,128)} all-reduce(f32[128,2]{0,1:T(2,128)S(1)} %get-tuple-element.16), channel_id=1, replica_groups=mesh['fsdp'=8,'ep'=4] {'ep'}, use_global_device_ids=true, to_apply=%region_7.0 | all-reduce | flops 256 | bytes 2048 | tf_op jit(solution)/shard_map/psum | solution.py:46
  259.0 0.0 copy-done.1
  259.0 1.5 convolution_convert_fusion
  260.5 11.4 %convert_bitcast_fusion = bf16[768,2,2048]{0,2,1:T(8,128)(2,1)} fusion(bf16[1024,2,2048]{2,0,1:T(8,128)(2,1)} %all-gather.3.cloned.1.call-done, bf16[1024,768,1]{1,0,2:T(8,128)(2,1)} %bitcast.35), kind=kOutput, calls=%fused_computation | convolution fusion | flops 6445596672 | bytes 16252928 | tf_op jit(solution)/shard_map/td,tef->def/dot_general | solution.py:40
  271.9 16.3 %copy.36 = bf16[768,2,2048]{2,1,0:T(2,128)(2,1)} copy(bf16[768,2,2048]{0,2,1:T(8,128)(2,1)} %convert_bitcast_fusion) | data formatting | bytes 12582912
  288.2 0.0 reduce-scatter.3.cloned.1.call-done
  (5 shorter events, 0.1 us)
Async XLA Ops:
  7.2 145.7 %copy-start = (bf16[256,2048]{1,0:T(8,128)(2,1)S(1)}, bf16[256,2048]{1,0:T(8,128)(2,1)}, u32[]{:S(2)}) copy-start(bf16[256,2048]{1,0:T(8,128)(2,1)} %param.5) | copy-start | bytes 3145732
  7.2 40.7 %all-gather.5.cloned.1.call-start = ((), (), s32[]{:S(2)}) async-start(), calls=%async_computation.6 | async-start | bytes 1966080 | tf_op jit(solution)/shard_map/all_gather | solution.py:33
  7.9 144.9 %reduce-scatter.5.cloned.1.call-start = ((), (), s32[]{:S(2)}) async-start(), calls=%async_computation.7 | async-start | bytes 9437184 | tf_op jit(solution)/shard_map/reduce_scatter | solution.py:36
  47.9 26.5 %copy-start.5 = (bf16[768,2,2048]{2,1,0:T(2,128)(2,1)S(1)}, bf16[768,2,2048]{2,1,0:T(2,128)(2,1)}, u32[]{:S(2)}) copy-start(bf16[768,2,2048]{2,1,0:T(2,128)(2,1)} %param.6) | copy-start | bytes 18874372
  73.2 1.1 copy-start.2
  83.6 0.7 copy-start.3
  83.6 71.1 %copy-start.4 = (f32[128,2]{0,1:T(2,128)S(1)}, f32[128,2]{0,1:T(2,128)}, u32[]{:S(2)}) copy-start(f32[128,2]{0,1:T(2,128)} %param.8) | copy-start | bytes 3076
  83.6 126.5 %all-gather.3.cloned.1.call-start = ((), (), s32[]{:S(2)}) async-start(), calls=%async_computation.4 | async-start | bytes 9437184 | tf_op jit(solution)/shard_map/all_gather | solution.py:32
  155.9 132.4 %reduce-scatter.3.cloned.1.call-start = ((), (), s32[]{:S(2)}) async-start(), calls=%async_computation.5 | async-start | bytes 1966080 | tf_op jit(solution)/shard_map/reduce_scatter | solution.py:39
  245.1 13.9 %copy-start.1 = (bf16[128,2,2048]{2,0,1:T(8,128)(2,1)S(1)}, bf16[128,2,2048]{2,0,1:T(8,128)(2,1)}, u32[]{:S(2)}) copy-start(bf16[128,2,2048]{2,0,1:T(8,128)(2,1)} %reduce-scatter.5.cloned.1.call-done) | copy-start | bytes 3145732
Sparse Core Ops, SparseCore 0:
  9.6 38.2 all-gather.4
  83.7 69.1 reduce-scatter.4
  156.0 54.1 all-gather.2
  246.6 35.3 reduce-scatter.2

commit v2 on v1

v2 whole, which is shorter than its diff:
```python
import functools

import jax
import jax.numpy as jnp
from jax import lax
from jax.experimental import pallas as pl
from jax.experimental.layout import Layout, with_layout_constraint
from jax.experimental.pallas import tpu as pltpu
from jax.sharding import PartitionSpec as P

F32 = jnp.float32
BF16 = jnp.bfloat16
MESH = pl.DeviceIdType.MESH
VMEM = pl.BlockSpec(memory_space=pltpu.VMEM)


def meet(n_fsdp, n_ep, p, z):
    barrier = pltpu.get_barrier_semaphore()
    for s in range(1, n_ep):
        pl.semaphore_signal(
            barrier, inc=1, device_id=(p, lax.rem(z + s, n_ep)), device_id_type=MESH
        )
    for s in range(1, n_fsdp):
        pl.semaphore_signal(
            barrier, inc=1, device_id=(lax.rem(p + s, n_fsdp), z), device_id_type=MESH
        )
    pl.semaphore_wait(barrier, n_ep - 1 + n_fsdp - 1)


def remote(src, dst, send, recv, to):
    return pltpu.make_async_remote_copy(
        src_ref=src, dst_ref=dst, send_sem=send, recv_sem=recv, device_id=to, device_id_type=MESH
    )


def spread_kernel(n_fsdp, n_ep, g_ref, out_ref, held, zsend, zrecv, psend, precv):
    ratio = g_ref.shape[0]
    p, z = lax.axis_index("fsdp"), lax.axis_index("ep")
    meet(n_fsdp, n_ep, p, z)
    along = []
    for s in range(1, n_ep):
        copy = remote(g_ref, held.at[z], zsend.at[s], zrecv.at[z], (p, lax.rem(z + s, n_ep)))
        copy.start()
        along.append(copy)
    for s in range(n_ep):
        q = lax.rem(z + n_ep - s, n_ep)
        if s:
            remote(g_ref, held.at[q], zsend.at[s], zrecv.at[q], (p, z)).wait_recv()
        for r in range(ratio):
            block = held.at[q, r] if s else g_ref.at[r]
            i = q * ratio + r

            @pl.when(i != p)
            def _():
                remote(block, out_ref.at[p], psend.at[s, r], precv.at[p], (i, z)).start()

            @pl.when(i == p)
            def _():
                out_ref[p] = block[...]

    for s in range(n_ep):
        q = lax.rem(z + n_ep - s, n_ep)
        for r in range(ratio):
            block = held.at[q, r] if s else g_ref.at[r]
            i = q * ratio + r

            @pl.when(i != p)
            def _():
                remote(block, out_ref.at[p], psend.at[s, r], precv.at[p], (i, z)).wait_send()

    for s in range(1, n_fsdp):
        f = lax.rem(p + s, n_fsdp)
        remote(g_ref.at[0], out_ref.at[f], psend.at[0, 0], precv.at[f], (f, z)).wait_recv()
    for copy in along:
        copy.wait_send()


def collect_kernel(n_fsdp, n_ep, part_ref, out_ref, held, sums, psend, precv, zsend, zrecv):
    ratio = out_ref.shape[0]
    p, z = lax.axis_index("fsdp"), lax.axis_index("ep")
    meet(n_fsdp, n_ep, p, z)
    held[p] = part_ref[p]
    across = []
    for s in range(1, n_fsdp):
        i = lax.rem(p + s, n_fsdp)
        copy = remote(part_ref.at[i], held.at[p], psend.at[s], precv.at[p], (i, z))
        copy.start()
        across.append(copy)
    along = []
    for s in range(1, n_ep + 1):
        q = lax.rem(z + s, n_ep)
        for r in range(ratio):
            f = q * ratio + r

            @pl.when(f != p)
            def _():
                remote(part_ref.at[0], held.at[f], psend.at[0], precv.at[f], (p, z)).wait_recv()

        if s < n_ep:
            copy = remote(
                held.at[pl.ds(q * ratio, ratio)], sums.at[z], zsend.at[s], zrecv.at[z], (p, q)
            )
            copy.start()
            along.append(copy)
    total = held[pl.ds(z * ratio, ratio)].astype(F32)
    for s in range(1, n_ep):
        q = lax.rem(z + s, n_ep)
        remote(
            held.at[pl.ds(q * ratio, ratio)], sums.at[q], zsend.at[s], zrecv.at[q], (p, q)
        ).wait_recv()
        total = total + sums[q].astype(F32)
    out_ref[...] = total.astype(BF16)
    for copy in across + along:
        copy.wait_send()


def add_kernel(n_ep, x_ref, out_ref, held, send, recv):
    p, z = lax.axis_index("fsdp"), lax.axis_index("ep")
    meet(1, n_ep, p, z)
    copies = []
    for s in range(1, n_ep):
        copy = remote(x_ref, held.at[z], send.at[s], recv.at[z], (p, lax.rem(z + s, n_ep)))
        copy.start()
        copies.append(copy)
    total = x_ref[...]
    for s in range(1, n_ep):
        q = lax.rem(z + s, n_ep)
        remote(x_ref, held.at[q], send.at[s], recv.at[q], (p, q)).wait_recv()
        total = total + held[q]
    out_ref[...] = total
    for copy in copies:
        copy.wait_send()


def talk(body, key, x, shape, scratch, flops=0):
    return pl.pallas_call(
        body,
        out_shape=jax.ShapeDtypeStruct(shape, x.dtype),
        in_specs=[VMEM],
        out_specs=VMEM,
        scratch_shapes=scratch,
        cost_estimate=pl.CostEstimate(flops=flops, bytes_accessed=100_000_000, transcendentals=0),
        compiler_params=pltpu.CompilerParams(collective_id=key, has_side_effects=True),
    )(x)


def spread(grad_out, n_fsdp, n_ep):
    tokens, width = grad_out.shape
    ratio = n_fsdp // n_ep
    cut = width // ratio
    blocks = jnp.stack([grad_out[:, r * cut : (r + 1) * cut] for r in range(ratio)])
    dma = pltpu.SemaphoreType.DMA
    out = talk(
        functools.partial(spread_kernel, n_fsdp, n_ep),
        0,
        blocks,
        (n_fsdp, tokens, cut),
        [
            pltpu.VMEM((n_ep, ratio, tokens, cut), BF16),
            dma((n_ep,)),
            dma((n_ep,)),
            dma((n_ep, ratio)),
            dma((n_fsdp,)),
        ],
    )
    return out.reshape(n_fsdp * tokens, cut)


def collect(part, n_fsdp, n_ep):
    cut = part.shape[1]
    tokens = part.shape[0] // n_fsdp
    ratio = n_fsdp // n_ep
    dma = pltpu.SemaphoreType.DMA
    out = talk(
        functools.partial(collect_kernel, n_fsdp, n_ep),
        1,
        part.reshape(n_fsdp, tokens, cut),
        (ratio, tokens, cut),
        [
            pltpu.VMEM((n_fsdp, tokens, cut), BF16),
            pltpu.VMEM((n_ep, ratio, tokens, cut), BF16),
            dma((n_fsdp,)),
            dma((n_fsdp,)),
            dma((n_ep,)),
            dma((n_ep,)),
        ],
    )
    return jnp.concatenate([out[r] for r in range(ratio)], axis=1)


def add_up(x, n_ep):
    dma = pltpu.SemaphoreType.DMA
    return talk(
        functools.partial(add_kernel, n_ep),
        2,
        x,
        x.shape,
        [pltpu.VMEM((n_ep,) + x.shape, F32), dma((n_ep,)), dma((n_ep,))],
    )


def route_maps(route_ids, probs, experts):
    tokens = route_ids.shape[0]
    names = jnp.arange(experts, dtype=jnp.int32)
    hits = (route_ids[:, :, None] == names[None, None, :]).astype(F32)
    named = jnp.sum(hits, axis=1)
    place = jnp.arange(tokens, dtype=jnp.int32)
    earlier = (place[None, :] < place[:, None]).astype(F32)
    rank = jnp.sum(earlier[:, :, None] * named[None, :, :], axis=1).astype(jnp.int32)
    token_prob = jnp.sum(hits * probs[:, :, None], axis=1)
    owns = (rank.T[:, :, None] == place[None, None, :]) & (named.T[:, :, None] > 0)
    return hits, token_prob, owns.astype(BF16)


def local(n_fsdp, n_ep, hidden, w_down, route_ids, probs, grad_out):
    rows, units = hidden.shape
    experts = w_down.shape[1]
    tokens = route_ids.shape[0]
    hits, token_prob, owns = route_maps(route_ids, probs, experts)
    hid_tok = jnp.einsum(
        "etr,erf->tef", owns, hidden.reshape(experts, tokens, units), preferred_element_type=F32
    )
    scaled = (token_prob[:, :, None] * hid_tok).astype(BF16)
    hid_tok = hid_tok.astype(BF16)
    hid_all = lax.all_gather(scaled, "fsdp", axis=0, tiled=True)
    grads = spread(grad_out, n_fsdp, n_ep)
    back_part = jnp.einsum("td,def->tef", grads, w_down, preferred_element_type=F32).astype(BF16)
    hid_all, back_part = lax.optimization_barrier((hid_all, back_part))
    back = lax.psum_scatter(back_part, "fsdp", scatter_dimension=0, tiled=True)
    part = jnp.einsum("tef,def->td", hid_all, w_down, preferred_element_type=F32).astype(BF16)
    output = collect(part, n_fsdp, n_ep)
    grad_weight = jnp.stack(
        [
            jnp.einsum("td,tf->df", grads, hid_all[:, e], preferred_element_type=F32).astype(BF16)
            for e in range(experts)
        ],
        axis=1,
    )
    grad_weight = with_layout_constraint(grad_weight, Layout(major_to_minor=(0, 1, 2)))
    back, output, grad_weight = lax.optimization_barrier((back, output, grad_weight))
    back = back.astype(F32)
    dots = jnp.sum(hid_tok.astype(F32) * back, axis=2)
    dots = add_up(dots.T, n_ep).T
    grad_tok = (token_prob[:, :, None] * back).astype(BF16)
    grad_hidden = jnp.einsum("etr,tef->erf", owns, grad_tok, preferred_element_type=F32)
    grad_hidden = grad_hidden.astype(BF16).reshape(rows, units)
    grad_probs = jnp.sum(hits * dots[:, None, :], axis=2)
    return (output, grad_hidden, grad_weight, grad_probs)


def solution(mesh):
    placed = (
        P("fsdp", "ep"),
        P("fsdp", None, "ep"),
        P("fsdp", None),
        P("fsdp", None),
        P("fsdp", "ep"),
    )
    return jax.shard_map(
        functools.partial(local, mesh.shape["fsdp"], mesh.shape["ep"]),
        mesh=mesh,
        in_specs=placed,
        out_specs=(P("fsdp", "ep"), P("fsdp", "ep"), P("fsdp", None, "ep"), P("fsdp", None)),
        check_vma=False,
    )
```

time: 298 us -> 237 us (0.80)
  waiting for transfers between devices: 163 us -> 12.3 us
  Pallas kernels: 0 us -> 120 us
  blocking collectives: 59.2 us -> 0 us
  other arithmetic: 1.31 us -> 21.2 us
  local copies, waits for them, and re-layouts: 21.1 us -> 27.3 us
  matrix products: 35.8 us -> 41 us
    pallas_call x0 -> x3, Pallas kernels: none -> 120 us  [talk(): pl.pallas_call(body, out_shape=jax.ShapeDtypeStruct(shape, x.dtype), in_s...]
    reduce_scatter x1, waiting for transfers between devices: 68.5 us -> 0.01 us  [local(): back = lax.psum_scatter(back_part, 'fsdp', scatter_dimension=0, tiled=True)]
    all_to_all x2 -> x0, blocking collectives: 46.6 us -> none  [the longest x1 23.7 us: local(): lax.all_to_all(grads, 'fsdp', split_axis=1, concat_axis=0, tiled=True)]
    all_gather x1, waiting for transfers between devices: 54.2 us -> 12.3 us  [local(): hid_all = lax.all_gather(scaled, 'fsdp', axis=0, tiled=True)]
    all_gather x1 -> x0, waiting for transfers between devices: 40 us -> none  [local(): grads = lax.all_gather(grad_out, 'ep', axis=1, tiled=True)]
    another operation x0 -> x3, local copies, waits for them, and re-layouts: none -> 26.9 us  [the longest x2 25.9 us: local(): jnp.stack([jnp.einsum('td,tf->df', grads, hid_all[:, e], preferred_elemen...]
    unnamed x13 -> x8, local copies, waits for them, and re-layouts: 18.1 us -> 0.29 us
    another operation x0 -> x2, other arithmetic: none -> 16.1 us  [the longest x1 15.3 us: local(): jnp.stack([jnp.einsum('td,tf->df', grads, hid_all[:, e], preferred_elemen...]
  transfers between devices with their start and end apart: 4 -> 2, of which waited for: 3 -> 1; matrix products, arithmetic and copies ran while one was open for 10% -> 34% of each run, Pallas kernels for 0% -> 45%
where the time goes in v2:
time: 237 us; the launch traced here: 236 us
  Pallas kernels  120 us (51%)
  matrix products  41 us (17%)
  local copies, waits for them, and re-layouts  27.3 us (12%)
  other arithmetic  21.2 us (9%)
  between operations  14.2 us (6%)
  waiting for transfers between devices  12.3 us (5%)
    pallas_call x3, Pallas kernels, talk(): pl.pallas_call(body, out_shape=jax.ShapeDtypeStruct(shape, x.dtype), in_s...  120 us
    another operation x2, local copies, waits for them, and re-layouts, local(): jnp.stack([jnp.einsum('td,tf->df', grads, hid_all[:, e], preferred_elemen...  25.9 us
    another operation x1, other arithmetic, local(): jnp.stack([jnp.einsum('td,tf->df', grads, hid_all[:, e], preferred_elemen...  15.3 us
    dot_general x1, matrix products, local(): jnp.einsum('tef,def->td', hid_all, w_down, preferred_element_type=F32)  12.8 us
    all_gather x1, waiting for transfers between devices, local(): hid_all = lax.all_gather(scaled, 'fsdp', axis=0, tiled=True)  12.3 us
    dot_general x2, matrix products, local(): jnp.einsum('td,tf->df', grads, hid_all[:, e], preferred_element_type=F32)  12.2 us
    dot_general x1, matrix products, local(): jnp.einsum('td,def->tef', grads, w_down, preferred_element_type=F32)  11.7 us
  transfers between devices with their start and end apart: 2, of which 1 were waited for; matrix products, arithmetic and copies ran while one was open for 34% of the time, Pallas kernels for 45%

profile of v2, /device:TPU:4, one launch (start us, length us, event | category | flops | bytes accessed | tf_op | source)
XLA Modules:
  0.0 236.4 jit_solution(1252679550055989156)
XLA Ops:
  7.2 0.0 copy-start
  7.2 0.0 all-gather.2.cloned.1.call-start
  7.2 0.8 select_reduce_fusion.1
  8.0 0.1 multiply_reduce_fusion
  8.2 0.3 copy-done
  8.4 1.5 multiply_convert_fusion
  9.9 0.0 all-gather.2.cloned.1.call-update
  9.9 0.0 reduce-scatter.2.cloned.1.call-start
  10.0 1.1 slice_bitcast_fusion.3
  11.0 0.8 pad_maximum_fusion.1.g_ref
  11.8 50.6 %shard_map.84 = bf16[8,128,768]{2,1,0:T(8,128)(2,1)} custom-call(bf16[2,128,768]{2,1,0:T(8,128)(2,1)} %pad_maximum_fusion.1.g_ref), custom_call_target="tpu_custom_call" | custom-call | bytes 100000000 | tf_op jit(solution)/shard_map/pallas_call | solution.py:136
  62.4 11.7 %fusion.4 = bf16[1024,2,2048]{2,0,1:T(8,128)(2,1)} fusion(bf16[1024,768,1]{1,0,2:T(8,128)(2,1)} %bitcast.48, bf16[768,2,2048]{2,1,0:T(2,128)(2,1)} %param.6), kind=kOutput, calls=%fused_computation.5 | convolution fusion | flops 6446645248 | bytes 16252928 | tf_op jit(solution)/shard_map/td,def->tef/dot_general | solution.py:227
  74.1 12.3 %all-gather.2.cloned.1.call-done = bf16[1024,2,2048]{2,0,1:T(8,128)(2,1)} async-done(((bf16[128,2,2048]{2,0,1:T(8,128)(2,1)}), bf16[1024,2,2048]{2,0,1:T(8,128)(2,1)}) %all-gather.2.cloned.1.call-update) | async-done | bytes 8388624 | tf_op jit(solution)/shard_map/all_gather | solution.py:225
  86.4 0.0 reduce-scatter.2.cloned.1.call-update
  86.5 12.8 %bitcast_convert_fusion = bf16[1024,768]{1,0:T(8,128)(2,1)} fusion(bf16[1024,2,2048]{2,0,1:T(8,128)(2,1)} %all-gather.2.cloned.1.call-done, bf16[768,2,2048]{2,1,0:T(2,128)(2,1)} %param.6), kind=kOutput, calls=%fused_computation.14 | convolution fusion | flops 6443237376 | bytes 16252928 | tf_op jit(solution)/shard_map/tef,def->td/dot_general | solution.py:230
  99.3 55.4 %shard_map.85 = bf16[2,128,768]{2,1,0:T(8,128)(2,1)} custom-call(bf16[8,128,768]{2,1,0:T(8,128)(2,1)} %bitcast.51), custom_call_target="tpu_custom_call" | custom-call | bytes 100000000 | tf_op jit(solution)/shard_map/pallas_call | solution.py:136
  154.7 6.1 %fusion.22 = bf16[768,1,2048]{2,0,1:T(8,128)(2,1)S(1)} fusion(bf16[1024,768]{1,0:T(8,128)(2,1)} %bitcast.49, bf16[1024,2,2048]{2,0,1:T(8,128)(2,1)} %all-gather.2.cloned.1.call-done), kind=kOutput, calls=%fused_computation.16 | convolution fusion | flops 3222798336 | bytes 8912896 | tf_op jit(solution)/shard_map/td,tf->df/dot_general | solution.py:234
  160.8 0.0 copy-start.1
  160.8 12.9 %copy.28 = bf16[768,1,2048]{2,1,0:T(2,128)(2,1)S(1)} copy(bf16[768,1,2048]{2,0,1:T(8,128)(2,1)S(1)} %fusion.22) | data formatting | bytes 6291456 | tf_op jit(solution)/shard_map/stack | solution.py:232
  173.8 0.0 copy-done.1
  173.8 6.1 %fusion.19 = bf16[768,1,2048]{2,0,1:T(8,128)(2,1)S(1)} fusion(bf16[1024,768]{1,0:T(8,128)(2,1)S(1)} %bitcast.50, bf16[1024,2,2048]{2,0,1:T(8,128)(2,1)} %all-gather.2.cloned.1.call-done), kind=kOutput, calls=%fused_computation.15 | convolution fusion | flops 3222798336 | bytes 8912896 | tf_op jit(solution)/shard_map/td,tf->df/dot_general | solution.py:234
  179.9 0.0 copy-start.2
  179.9 12.9 %copy.29 = bf16[768,1,2048]{2,1,0:T(2,128)(2,1)S(1)} copy(bf16[768,1,2048]{2,0,1:T(8,128)(2,1)S(1)} %fusion.19) | data formatting | bytes 6291456 | tf_op jit(solution)/shard_map/stack | solution.py:232
  192.9 0.0 copy-done.2
  192.9 0.8 pad_maximum_fusion.2
  193.7 0.0 copy-start.3
  193.7 15.3 %pad_maximum_fusion = bf16[768,2,2048]{2,1,0:T(2,128)(2,1)} fusion(bf16[768,1,2048]{2,1,0:T(2,128)(2,1)S(1)} %copy.29, bf16[768,1,2048]{2,1,0:T(2,128)(2,1)S(1)} %copy.28), kind=kLoop, calls=%fused_computation | loop fusion | flops 12582912 | bytes 12582912 | tf_op jit(solution)/shard_map/stack | solution.py:232
  209.0 0.0 reduce-scatter.2.cloned.1.call-done
  209.0 2.7 %convolution_convert_fusion = bf16[2,128,2048]{2,1,0:T(8,128)(2,1)} fusion(bf16[128,2,2048]{2,0,1:T(8,128)(2,1)} %reduce-scatter.2.cloned.1.call-done, f32[128,2]{0,1:T(2,128)S(1)} %get-tuple-element.14, s32[2,128]{1,0:T(2,128)S(1)} %convert_bitcast_fusion, pred[2,128]{1,0:T(4,128)(4,1)S(1)} %compare_bitcast_fusion), kind=kOutput, calls=%fused_computation.20 | convolution fusion | flops 136380416 | bytes 2099456 | tf_op jit(solution)/shard_map/etr,tef->erf/dot_general | solution.py:245
  211.7 2.2 fusion.26
  213.8 14.4 %shard_map.86 = f32[2,128]{1,0:T(2,128)} custom-call(f32[2,128]{1,0:T(2,128)} %bitcast.53), custom_call_target="tpu_custom_call" | custom-call | bytes 100000000 | tf_op jit(solution)/shard_map/pallas_call | solution.py:136
  228.3 0.0 copy-done.3
  228.3 1.3 select_reduce_fusion
  (4 shorter events, 0.1 us)
Async XLA Ops:
  7.2 1.3 copy-start
  7.2 79.2 %all-gather.2.cloned.1.call-start = ((), (), s32[]{:S(2)}) async-start(), calls=%async_computation.1 | async-start | bytes 9437184 | tf_op jit(solution)/shard_map/all_gather | solution.py:225
  9.9 199.1 %reduce-scatter.2.cloned.1.call-start = ((), (), s32[]{:S(2)}) async-start(), calls=%async_computation.2 | async-start | bytes 9437184 | tf_op jit(solution)/shard_map/reduce_scatter | solution.py:229
  160.8 13.0 %copy-start.1 = (bf16[8,128,768]{2,1,0:T(8,128)(2,1)S(1)}, bf16[8,128,768]{2,1,0:T(8,128)(2,1)}, u32[]{:S(2)}) copy-start(bf16[8,128,768]{2,1,0:T(8,128)(2,1)} %shard_map.84) | copy-start | bytes 4718596
  179.9 13.0 %copy-start.2 = (bf16[2,128,768]{2,1,0:T(8,128)(2,1)S(1)}, bf16[2,128,768]{2,1,0:T(8,128)(2,1)}, u32[]{:S(2)}) copy-start(bf16[2,128,768]{2,1,0:T(8,128)(2,1)} %shard_map.85) | copy-start | bytes 1179652
  193.7 34.6 %copy-start.3 = (s32[128,2]{0,1:T(2,128)S(1)}, s32[128,2]{0,1:T(2,128)}, u32[]{:S(2)}) copy-start(s32[128,2]{0,1:T(2,128)} %param.7) | copy-start | bytes 3076
Sparse Core Ops, SparseCore 0:
  10.5 75.8 all-gather.1
  89.9 82.2 reduce-scatter.1

commit v3 on v2

--- a/solution.py
+++ b/solution.py
@@ -33,32 +33,24 @@
     )
 
 
-def spread_kernel(n_fsdp, n_ep, g_ref, out_ref, held, zsend, zrecv, psend, precv):
+def spread_kernel(
+    n_fsdp, n_ep, g_ref, h_ref, out_ref, hall_ref, held, zsend, zrecv, psend, precv, hsend, fsend, hrecv, own
+):
     ratio = g_ref.shape[0]
+    n_chip = n_fsdp // 2
     p, z = lax.axis_index("fsdp"), lax.axis_index("ep")
+    chip, core = lax.div(p, 2), lax.rem(p, 2)
+    mate = chip * 2 + 1 - core
     meet(n_fsdp, n_ep, p, z)
-    along = []
+    sends = []
     for s in range(1, n_ep):
         copy = remote(g_ref, held.at[z], zsend.at[s], zrecv.at[z], (p, lax.rem(z + s, n_ep)))
         copy.start()
-        along.append(copy)
-    for s in range(n_ep):
-        q = lax.rem(z + n_ep - s, n_ep)
-        if s:
-            remote(g_ref, held.at[q], zsend.at[s], zrecv.at[q], (p, z)).wait_recv()
-        for r in range(ratio):
-            block = held.at[q, r] if s else g_ref.at[r]
-            i = q * ratio + r
-
-            @pl.when(i != p)
-            def _():
-                remote(block, out_ref.at[p], psend.at[s, r], precv.at[p], (i, z)).start()
-
-            @pl.when(i == p)
-            def _():
-                out_ref[p] = block[...]
-
-    for s in range(n_ep):
+        sends.append(copy)
+    keep = pltpu.make_async_copy(h_ref, hall_ref.at[:, p], own)
+    keep.start()
+
+    def pieces(s, act):
         q = lax.rem(z + n_ep - s, n_ep)
         for r in range(ratio):
             block = held.at[q, r] if s else g_ref.at[r]
@@ -66,13 +58,51 @@
 
             @pl.when(i != p)
             def _():
-                remote(block, out_ref.at[p], psend.at[s, r], precv.at[p], (i, z)).wait_send()
-
+                act(remote(block, out_ref.at[p], psend.at[s, r], precv.at[p], (i, z)))
+
+            if act is begin:
+
+                @pl.when(i == p)
+                def _():
+                    out_ref[p] = block[...]
+
+    def begin(copy):
+        copy.start()
+
+    def end(copy):
+        copy.wait_send()
+
+    pieces(0, begin)
+    for s in range(1, n_chip):
+        to = lax.rem(chip + s, n_chip) * 2 + core
+        copy = remote(h_ref, hall_ref.at[:, p], hsend.at[s], hrecv.at[p], (to, z))
+        copy.start()
+        sends.append(copy)
+    copy = remote(h_ref, hall_ref.at[:, p], hsend.at[0], hrecv.at[p], (mate, z))
+    copy.start()
+    sends.append(copy)
+    for s in range(1, max(n_ep, n_chip)):
+        if s < n_ep:
+            q = lax.rem(z + n_ep - s, n_ep)
+            remote(g_ref, held.at[q], zsend.at[s], zrecv.at[q], (p, z)).wait_recv()
+            pieces(s, begin)
+        if s < n_chip:
+            f = lax.rem(chip + n_chip - s, n_chip) * 2 + core
+            copy = remote(hall_ref.at[:, f], hall_ref.at[:, f], fsend.at[s], hrecv.at[f], (mate, z))
+            copy.wait_recv()
+            copy.start()
+            sends.append(copy)
+    for s in range(n_chip):
+        f = lax.rem(chip + s, n_chip) * 2 + 1 - core
+        remote(h_ref, hall_ref.at[:, f], hsend.at[0], hrecv.at[f], (mate, z)).wait_recv()
     for s in range(1, n_fsdp):
         f = lax.rem(p + s, n_fsdp)
         remote(g_ref.at[0], out_ref.at[f], psend.at[0, 0], precv.at[f], (f, z)).wait_recv()
-    for copy in along:
-        copy.wait_send()
+    for s in range(n_ep):
+        pieces(s, end)
+    for copy in sends:
+        copy.wait_send()
+    keep.wait()
 
 
 def collect_kernel(n_fsdp, n_ep, part_ref, out_ref, held, sums, psend, precv, zsend, zrecv):
@@ -144,26 +174,36 @@
     )(x)
 
 
-def spread(grad_out, n_fsdp, n_ep):
+def spread(grad_out, scaled, n_fsdp, n_ep):
     tokens, width = grad_out.shape
+    experts, _, units = scaled.shape
     ratio = n_fsdp // n_ep
     cut = width // ratio
     blocks = jnp.stack([grad_out[:, r * cut : (r + 1) * cut] for r in range(ratio)])
     dma = pltpu.SemaphoreType.DMA
-    out = talk(
+    anywhere = pl.BlockSpec(memory_space=pl.ANY)
+    out, hid_all = pl.pallas_call(
         functools.partial(spread_kernel, n_fsdp, n_ep),
-        0,
-        blocks,
-        (n_fsdp, tokens, cut),
-        [
+        out_shape=(
+            jax.ShapeDtypeStruct((n_fsdp, tokens, cut), BF16),
+            jax.ShapeDtypeStruct((experts, n_fsdp, tokens, units), BF16),
+        ),
+        in_specs=[VMEM, anywhere],
+        out_specs=(VMEM, anywhere),
+        scratch_shapes=[
             pltpu.VMEM((n_ep, ratio, tokens, cut), BF16),
             dma((n_ep,)),
             dma((n_ep,)),
             dma((n_ep, ratio)),
             dma((n_fsdp,)),
+            dma((n_fsdp // 2,)),
+            dma((n_fsdp // 2,)),
+            dma((n_fsdp,)),
+            dma,
         ],
-    )
-    return out.reshape(n_fsdp * tokens, cut)
+        compiler_params=pltpu.CompilerParams(collective_id=0, has_side_effects=True),
+    )(blocks, scaled)
+    return out.reshape(n_fsdp * tokens, cut), hid_all.reshape(experts, n_fsdp * tokens, units)
 
 
 def collect(part, n_fsdp, n_ep):
@@ -218,28 +258,21 @@
     tokens = route_ids.shape[0]
     hits, token_prob, owns = route_maps(route_ids, probs, experts)
     hid_tok = jnp.einsum(
-        "etr,erf->tef", owns, hidden.reshape(experts, tokens, units), preferred_element_type=F32
-    )
-    scaled = (token_prob[:, :, None] * hid_tok).astype(BF16)
+        "etr,erf->etf", owns, hidden.reshape(experts, tokens, units), preferred_element_type=F32
+    )
+    scaled = (token_prob.T[:, :, None] * hid_tok).astype(BF16)
     hid_tok = hid_tok.astype(BF16)
-    hid_all = lax.all_gather(scaled, "fsdp", axis=0, tiled=True)
-    grads = spread(grad_out, n_fsdp, n_ep)
+    grads, hid_all = spread(grad_out, scaled, n_fsdp, n_ep)
     back_part = jnp.einsum("td,def->tef", grads, w_down, preferred_element_type=F32).astype(BF16)
     hid_all, back_part = lax.optimization_barrier((hid_all, back_part))
     back = lax.psum_scatter(back_part, "fsdp", scatter_dimension=0, tiled=True)
-    part = jnp.einsum("tef,def->td", hid_all, w_down, preferred_element_type=F32).astype(BF16)
+    part = jnp.einsum("etf,def->td", hid_all, w_down, preferred_element_type=F32).astype(BF16)
     output = collect(part, n_fsdp, n_ep)
-    grad_weight = jnp.stack(
-        [
-            jnp.einsum("td,tf->df", grads, hid_all[:, e], preferred_element_type=F32).astype(BF16)
-            for e in range(experts)
-        ],
-        axis=1,
-    )
+    grad_weight = jnp.einsum("td,etf->def", grads, hid_all, preferred_element_type=F32).astype(BF16)
     grad_weight = with_layout_constraint(grad_weight, Layout(major_to_minor=(0, 1, 2)))
     back, output, grad_weight = lax.optimization_barrier((back, output, grad_weight))
     back = back.astype(F32)
-    dots = jnp.sum(hid_tok.astype(F32) * back, axis=2)
+    dots = jnp.sum(hid_tok.transpose(1, 0, 2).astype(F32) * back, axis=2)
     dots = add_up(dots.T, n_ep).T
     grad_tok = (token_prob[:, :, None] * back).astype(BF16)
     grad_hidden = jnp.einsum("etr,tef->erf", owns, grad_tok, preferred_element_type=F32)

time: 237 us -> 224 us (0.945)
  Pallas kernels: 120 us -> 144 us
  other arithmetic: 21.2 us -> 5.87 us
  waiting for transfers between devices: 12.3 us -> 0.02 us
  local copies, waits for them, and re-layouts: 27.3 us -> 20.9 us
  matrix products: 41 us -> 38.5 us
    pallas_call x0 -> x1, Pallas kernels: none -> 68.2 us  [spread(): pl.pallas_call(functools.partial(spread_kernel, n_fsdp, n_ep), out_shape=...]
    pallas_call x3 -> x2, Pallas kernels: 120 us -> 75.7 us  [talk(): pl.pallas_call(body, out_shape=jax.ShapeDtypeStruct(shape, x.dtype), in_s...]
    another operation x2 -> x0, local copies, waits for them, and re-layouts: 25.9 us -> none  [local(): jnp.stack([jnp.einsum('td,tf->df', grads, hid_all[:, e], preferred_elemen...]
    dot_general x0 -> x1, local copies, waits for them, and re-layouts: none -> 18.8 us  [local(): jnp.einsum('td,etf->def', grads, hid_all, preferred_element_type=F32)]
    another operation x1 -> x0, other arithmetic: 15.3 us -> none  [local(): jnp.stack([jnp.einsum('td,tf->df', grads, hid_all[:, e], preferred_elemen...]
    all_gather x1 -> x0, waiting for transfers between devices: 12.3 us -> none  [local(): hid_all = lax.all_gather(scaled, 'fsdp', axis=0, tiled=True)]
    dot_general x4 -> x3, matrix products: 26.5 us -> 24 us  [the longest x1 12.9 us: local(): jnp.einsum('etf,def->td', hid_all, w_down, preferred_element_type=F32)]
  transfers between devices with their start and end apart: 2 -> 1, of which waited for: 1 -> 0; matrix products, arithmetic and copies ran while one was open for 34% -> 19% of each run, Pallas kernels for 45% -> 27%
where the time goes in v3:
time: 224 us; the launch traced here: 223 us
  Pallas kernels  144 us (64%)
  matrix products  38.5 us (17%)
  local copies, waits for them, and re-layouts  20.9 us (9%)
  between operations  14.1 us (6%)
  other arithmetic  5.87 us (3%)
    pallas_call x2, Pallas kernels, talk(): pl.pallas_call(body, out_shape=jax.ShapeDtypeStruct(shape, x.dtype), in_s...  75.7 us
    pallas_call x1, Pallas kernels, spread(): pl.pallas_call(functools.partial(spread_kernel, n_fsdp, n_ep), out_shape=...  68.2 us
    dot_general x1, local copies, waits for them, and re-layouts, local(): jnp.einsum('td,etf->def', grads, hid_all, preferred_element_type=F32)  18.8 us
    dot_general x1, matrix products, local(): jnp.einsum('etf,def->td', hid_all, w_down, preferred_element_type=F32)  12.9 us
    dot_general x1, matrix products, local(): jnp.einsum('td,def->tef', grads, w_down, preferred_element_type=F32)  11.8 us
    dot_general x1, matrix products, local(): jnp.einsum('td,etf->def', grads, hid_all, preferred_element_type=F32)  9.67 us
  transfers between devices with their start and end apart: 1, of which 0 were waited for; matrix products, arithmetic and copies ran while one was open for 19% of the time, Pallas kernels for 27%

profile of v3, /device:TPU:4, one launch (start us, length us, event | category | flops | bytes accessed | tf_op | source)
XLA Modules:
  0.0 223.3 jit_solution(13023023352624296490)
XLA Ops:
  7.2 0.0 copy-start
  7.2 0.0 reduce-scatter.2.cloned.1.call-start
  7.2 0.8 select_reduce_fusion.1
  8.0 0.1 multiply_reduce_fusion
  8.2 1.1 slice_bitcast_fusion.3
  9.2 0.8 pad_maximum_fusion.g_ref
  10.0 0.0 copy-done
  10.0 1.5 multiply_convert_fusion
  11.5 68.2 %shard_map.84 = (bf16[8,128,768]{2,1,0:T(8,128)(2,1)}, bf16[2,8,128,2048]{3,2,1,0:T(8,128)(2,1)}) custom-call(bf16[2,128,768]{2,1,0:T(8,128)(2,1)} %pad_maximum_fusion.g_ref, bf16[2,128,2048]{2,1,0:T(8,128)(2,1)} %get-tuple-element.24.h_ref), custom_call_target="tpu_custom_call" | custom-call | tf_op jit(solution)/shard_map/pallas_call | solution.py:185
  79.6 11.8 %fusion.4 = bf16[1024,2,2048]{2,0,1:T(8,128)(2,1)} fusion(bf16[1024,768,1]{1,0,2:T(8,128)(2,1)} %bitcast.40, bf16[768,2,2048]{2,1,0:T(2,128)(2,1)} %param.6), kind=kOutput, calls=%fused_computation.5 | convolution fusion | flops 6446645248 | bytes 16252928 | tf_op jit(solution)/shard_map/td,def->tef/dot_general | solution.py:266
  91.4 0.0 reduce-scatter.2.cloned.1.call-update
  91.4 9.7 %fusion.22 = bf16[768,2,2048]{2,0,1:T(8,128)(2,1)S(1)} fusion(bf16[1024,768,1]{1,0,2:T(8,128)(2,1)} %bitcast.41, bf16[2,1024,2048]{2,1,0:T(8,128)(2,1)} %bitcast.38), kind=kOutput, calls=%fused_computation.36 | convolution fusion | flops 6442450944 | bytes 16252928 | tf_op jit(solution)/shard_map/td,etf->def/dot_general | solution.py:271
  101.1 18.8 %copy.35 = bf16[768,2,2048]{2,1,0:T(2,128)(2,1)} copy(bf16[768,2,2048]{2,0,1:T(8,128)(2,1)S(1)} %fusion.22) | data formatting | bytes 12582912 | tf_op jit(solution)/shard_map/td,etf->def/dot_general | solution.py:271
  119.9 12.9 %bitcast_convert_fusion = bf16[1024,768]{1,0:T(8,128)(2,1)} fusion(bf16[2,1024,2048]{2,1,0:T(8,128)(2,1)} %bitcast.39, bf16[768,2,2048]{2,1,0:T(2,128)(2,1)} %param.6), kind=kOutput, calls=%fused_computation.6 | convolution fusion | flops 6443237376 | bytes 16252928 | tf_op jit(solution)/shard_map/etf,def->td/dot_general | solution.py:269
  132.7 0.0 copy-start.1
  132.7 61.4 %shard_map.85 = bf16[2,128,768]{2,1,0:T(8,128)(2,1)} custom-call(bf16[8,128,768]{2,1,0:T(8,128)(2,1)} %bitcast.33), custom_call_target="tpu_custom_call" | custom-call | bytes 100000000 | tf_op jit(solution)/shard_map/pallas_call | solution.py:166
  194.1 1.0 slice_bitcast_fusion.1
  195.2 0.8 pad_maximum_fusion.1
  196.0 0.0 reduce-scatter.2.cloned.1.call-done
  196.0 2.7 %convolution_convert_fusion = bf16[2,128,2048]{2,1,0:T(8,128)(2,1)} fusion(bf16[128,2,2048]{2,0,1:T(8,128)(2,1)} %reduce-scatter.2.cloned.1.call-done, f32[128,2]{0,1:T(2,128)S(1)} %get-tuple-element.18, s32[2,128]{1,0:T(2,128)S(1)} %convert_bitcast_fusion, pred[2,128]{1,0:T(4,128)(4,1)S(1)} %compare_bitcast_fusion), kind=kOutput, calls=%fused_computation.9 | convolution fusion | flops 136380416 | bytes 2099456 | tf_op jit(solution)/shard_map/etr,tef->erf/dot_general | solution.py:278
  198.7 2.1 fusion.8
  200.8 14.4 %shard_map.86 = f32[2,128]{1,0:T(2,128)} custom-call(f32[2,128]{1,0:T(2,128)} %bitcast.36), custom_call_target="tpu_custom_call" | custom-call | bytes 100000000 | tf_op jit(solution)/shard_map/pallas_call | solution.py:166
  215.2 0.0 copy-done.1
  215.2 1.3 select_reduce_fusion
  (3 shorter events, 0.0 us)
Async XLA Ops:
  7.2 2.8 %copy-start = (bf16[256,2048]{1,0:T(8,128)(2,1)S(1)}, bf16[256,2048]{1,0:T(8,128)(2,1)}, u32[]{:S(2)}) copy-start(bf16[256,2048]{1,0:T(8,128)(2,1)} %param.5) | copy-start | bytes 3145732
  7.2 188.8 %reduce-scatter.2.cloned.1.call-start = ((), (), s32[]{:S(2)}) async-start(), calls=%async_computation.1 | async-start | bytes 9437184 | tf_op jit(solution)/shard_map/reduce_scatter | solution.py:268
  132.7 82.4 %copy-start.1 = (s32[128,2]{0,1:T(2,128)S(1)}, s32[128,2]{0,1:T(2,128)}, u32[]{:S(2)}) copy-start(s32[128,2]{0,1:T(2,128)} %param.7) | copy-start | bytes 3076
Sparse Core Ops, SparseCore 0:
  91.6 91.7 reduce-scatter.1

commit v4 on v3

--- a/solution.py
+++ b/solution.py
@@ -41,6 +41,12 @@
     p, z = lax.axis_index("fsdp"), lax.axis_index("ep")
     chip, core = lax.div(p, 2), lax.rem(p, 2)
     mate = chip * 2 + 1 - core
+    rows_half = h_ref.shape[1] // 2
+
+    def around(c):
+        wide = n_chip // 2
+        return c + lax.div(c, wide) * (3 * wide - 1 - 2 * c)
+
     meet(n_fsdp, n_ep, p, z)
     sends = []
     for s in range(1, n_ep):
@@ -73,28 +79,41 @@
         copy.wait_send()
 
     pieces(0, begin)
-    for s in range(1, n_chip):
-        to = lax.rem(chip + s, n_chip) * 2 + core
-        copy = remote(h_ref, hall_ref.at[:, p], hsend.at[s], hrecv.at[p], (to, z))
-        copy.start()
-        sends.append(copy)
-    copy = remote(h_ref, hall_ref.at[:, p], hsend.at[0], hrecv.at[p], (mate, z))
-    copy.start()
-    sends.append(copy)
+    place = around(chip)
+    after = around(lax.rem(place + 1, n_chip)) * 2 + core
+    before = around(lax.rem(place + n_chip - 1, n_chip)) * 2 + core
+
+    def relay(s):
+        for half, to in ((0, after), (1, before)):
+            step = n_chip - s if half == 0 else s
+            f = around(lax.rem(place + step, n_chip)) * 2 + core
+            rows = pl.ds(half * rows_half, rows_half)
+            there = hall_ref.at[:, f, rows]
+            src = there if s else h_ref.at[:, rows]
+            if s:
+                remote(src, there, hsend.at[half, s], hrecv.at[half, f], (to, z)).wait_recv()
+            if s < n_chip - 1:
+                copy = remote(src, there, hsend.at[half, s], hrecv.at[half, f], (to, z))
+                copy.start()
+                sends.append(copy)
+            copy = remote(src, there, fsend.at[half, s], hrecv.at[half, f], (mate, z))
+            copy.start()
+            sends.append(copy)
+
+    relay(0)
     for s in range(1, max(n_ep, n_chip)):
+        if s < n_chip:
+            relay(s)
         if s < n_ep:
             q = lax.rem(z + n_ep - s, n_ep)
             remote(g_ref, held.at[q], zsend.at[s], zrecv.at[q], (p, z)).wait_recv()
             pieces(s, begin)
-        if s < n_chip:
-            f = lax.rem(chip + n_chip - s, n_chip) * 2 + core
-            copy = remote(hall_ref.at[:, f], hall_ref.at[:, f], fsend.at[s], hrecv.at[f], (mate, z))
-            copy.wait_recv()
-            copy.start()
-            sends.append(copy)
     for s in range(n_chip):
         f = lax.rem(chip + s, n_chip) * 2 + 1 - core
-        remote(h_ref, hall_ref.at[:, f], hsend.at[0], hrecv.at[f], (mate, z)).wait_recv()
+        for half in range(2):
+            rows = pl.ds(half * rows_half, rows_half)
+            there = hall_ref.at[:, f, rows]
+            remote(there, there, fsend.at[half, 0], hrecv.at[half, f], (mate, z)).wait_recv()
     for s in range(1, n_fsdp):
         f = lax.rem(p + s, n_fsdp)
         remote(g_ref.at[0], out_ref.at[f], psend.at[0, 0], precv.at[f], (f, z)).wait_recv()
@@ -196,9 +215,9 @@
             dma((n_ep,)),
             dma((n_ep, ratio)),
             dma((n_fsdp,)),
-            dma((n_fsdp // 2,)),
-            dma((n_fsdp // 2,)),
-            dma((n_fsdp,)),
+            dma((2, n_fsdp // 2)),
+            dma((2, n_fsdp // 2)),
+            dma((2, n_fsdp)),
             dma,
         ],
         compiler_params=pltpu.CompilerParams(collective_id=0, has_side_effects=True),

time: 224 us -> 229 us (1.022)
  Pallas kernels: 144 us -> 149 us
    pallas_call x1, Pallas kernels: 68.2 us -> 76.1 us  [spread(): pl.pallas_call(functools.partial(spread_kernel, n_fsdp, n_ep), out_shape=...]
    pallas_call x2, Pallas kernels: 75.7 us -> 73.3 us  [talk(): pl.pallas_call(body, out_shape=jax.ShapeDtypeStruct(shape, x.dtype), in_s...]
  transfers between devices with their start and end apart: 1 -> 1, of which waited for: 0 -> 0; matrix products, arithmetic and copies ran while one was open for 19% -> 19% of each run, Pallas kernels for 27% -> 26%
where the time goes in v4:
time: 229 us
  Pallas kernels  149 us (65%)
  matrix products  38.5 us (17%)
  local copies, waits for them, and re-layouts  20.9 us (9%)
  between operations  14.1 us (6%)
  other arithmetic  5.87 us (3%)
    pallas_call x1, Pallas kernels, spread(): pl.pallas_call(functools.partial(spread_kernel, n_fsdp, n_ep), out_shape=...  76.1 us
    pallas_call x2, Pallas kernels, talk(): pl.pallas_call(body, out_shape=jax.ShapeDtypeStruct(shape, x.dtype), in_s...  73.3 us
    dot_general x1, local copies, waits for them, and re-layouts, local(): jnp.einsum('td,etf->def', grads, hid_all, preferred_element_type=F32)  18.8 us
    dot_general x1, matrix products, local(): jnp.einsum('etf,def->td', hid_all, w_down, preferred_element_type=F32)  12.9 us
    dot_general x1, matrix products, local(): jnp.einsum('td,def->tef', grads, w_down, preferred_element_type=F32)  11.8 us
    dot_general x1, matrix products, local(): jnp.einsum('td,etf->def', grads, hid_all, preferred_element_type=F32)  9.67 us
  transfers between devices with their start and end apart: 1, of which 0 were waited for; matrix products, arithmetic and copies ran while one was open for 19% of the time, Pallas kernels for 26%

profile of v4, /device:TPU:4, one launch (start us, length us, event | category | flops | bytes accessed | tf_op | source)
XLA Modules:
  0.0 228.7 jit_solution(6444944194206777301)
XLA Ops:
  7.2 0.0 copy-start
  7.2 0.0 reduce-scatter.2.cloned.1.call-start
  7.2 0.8 select_reduce_fusion.1
  8.0 0.1 multiply_reduce_fusion
  8.2 1.1 slice_bitcast_fusion.3
  9.2 0.8 pad_maximum_fusion.g_ref
  10.0 0.0 copy-done
  10.0 1.5 multiply_convert_fusion
  11.5 76.1 %shard_map.84 = (bf16[8,128,768]{2,1,0:T(8,128)(2,1)}, bf16[2,8,128,2048]{3,2,1,0:T(8,128)(2,1)}) custom-call(bf16[2,128,768]{2,1,0:T(8,128)(2,1)} %pad_maximum_fusion.g_ref, bf16[2,128,2048]{2,1,0:T(8,128)(2,1)} %get-tuple-element.24.h_ref), custom_call_target="tpu_custom_call" | custom-call | tf_op jit(solution)/shard_map/pallas_call | solution.py:204
  87.6 11.8 %fusion.4 = bf16[1024,2,2048]{2,0,1:T(8,128)(2,1)} fusion(bf16[1024,768,1]{1,0,2:T(8,128)(2,1)} %bitcast.40, bf16[768,2,2048]{2,1,0:T(2,128)(2,1)} %param.6), kind=kOutput, calls=%fused_computation.5 | convolution fusion | flops 6446645248 | bytes 16252928 | tf_op jit(solution)/shard_map/td,def->tef/dot_general | solution.py:285
  99.3 0.0 reduce-scatter.2.cloned.1.call-update
  99.4 9.7 %fusion.22 = bf16[768,2,2048]{2,0,1:T(8,128)(2,1)S(1)} fusion(bf16[1024,768,1]{1,0,2:T(8,128)(2,1)} %bitcast.41, bf16[2,1024,2048]{2,1,0:T(8,128)(2,1)} %bitcast.38), kind=kOutput, calls=%fused_computation.36 | convolution fusion | flops 6442450944 | bytes 16252928 | tf_op jit(solution)/shard_map/td,etf->def/dot_general | solution.py:290
  109.0 18.8 %copy.35 = bf16[768,2,2048]{2,1,0:T(2,128)(2,1)} copy(bf16[768,2,2048]{2,0,1:T(8,128)(2,1)S(1)} %fusion.22) | data formatting | bytes 12582912 | tf_op jit(solution)/shard_map/td,etf->def/dot_general | solution.py:290
  127.8 12.9 %bitcast_convert_fusion = bf16[1024,768]{1,0:T(8,128)(2,1)} fusion(bf16[2,1024,2048]{2,1,0:T(8,128)(2,1)} %bitcast.39, bf16[768,2,2048]{2,1,0:T(2,128)(2,1)} %param.6), kind=kOutput, calls=%fused_computation.6 | convolution fusion | flops 6443237376 | bytes 16252928 | tf_op jit(solution)/shard_map/etf,def->td/dot_general | solution.py:288
  140.7 0.0 copy-start.1
  140.7 58.9 %shard_map.85 = bf16[2,128,768]{2,1,0:T(8,128)(2,1)} custom-call(bf16[8,128,768]{2,1,0:T(8,128)(2,1)} %bitcast.33), custom_call_target="tpu_custom_call" | custom-call | bytes 100000000 | tf_op jit(solution)/shard_map/pallas_call | solution.py:185
  199.6 1.0 slice_bitcast_fusion.1
  200.6 0.8 pad_maximum_fusion.1
  201.4 0.0 reduce-scatter.2.cloned.1.call-done
  201.4 2.7 %convolution_convert_fusion = bf16[2,128,2048]{2,1,0:T(8,128)(2,1)} fusion(bf16[128,2,2048]{2,0,1:T(8,128)(2,1)} %reduce-scatter.2.cloned.1.call-done, f32[128,2]{0,1:T(2,128)S(1)} %get-tuple-element.18, s32[2,128]{1,0:T(2,128)S(1)} %convert_bitcast_fusion, pred[2,128]{1,0:T(4,128)(4,1)S(1)} %compare_bitcast_fusion), kind=kOutput, calls=%fused_computation.9 | convolution fusion | flops 136380416 | bytes 2099456 | tf_op jit(solution)/shard_map/etr,tef->erf/dot_general | solution.py:297
  204.1 2.1 fusion.8
  206.3 14.4 %shard_map.86 = f32[2,128]{1,0:T(2,128)} custom-call(f32[2,128]{1,0:T(2,128)} %bitcast.36), custom_call_target="tpu_custom_call" | custom-call | bytes 100000000 | tf_op jit(solution)/shard_map/pallas_call | solution.py:185
  220.6 0.0 copy-done.1
  220.6 1.3 select_reduce_fusion
  (3 shorter events, 0.0 us)
Async XLA Ops:
  7.2 2.8 %copy-start = (bf16[256,2048]{1,0:T(8,128)(2,1)S(1)}, bf16[256,2048]{1,0:T(8,128)(2,1)}, u32[]{:S(2)}) copy-start(bf16[256,2048]{1,0:T(8,128)(2,1)} %param.5) | copy-start | bytes 3145732
  7.2 194.2 %reduce-scatter.2.cloned.1.call-start = ((), (), s32[]{:S(2)}) async-start(), calls=%async_computation.1 | async-start | bytes 9437184 | tf_op jit(solution)/shard_map/reduce_scatter | solution.py:287
  140.7 80.0 %copy-start.1 = (s32[128,2]{0,1:T(2,128)S(1)}, s32[128,2]{0,1:T(2,128)}, u32[]{:S(2)}) copy-start(s32[128,2]{0,1:T(2,128)} %param.7) | copy-start | bytes 3076
Sparse Core Ops, SparseCore 0:
  99.5 90.6 reduce-scatter.1
